TPU v7x, 32 devices: a whole 2x2x4 slice. The times are simulated.
32 devices in a mesh: src: 4 (over z), delay: 8 (over y, x, core).
Axes of the slice: x: 2, y: 2, z: 4, core: 2. Of those that a mesh axis runs over, the one named last changes fastest.
Arguments:
- history: float32 [32, 16, 16, 128], P('delay', 'src'), may hold values from -6 to 6
- slot_map: int32 [32], P('delay'), may hold values from 0 to 3, as said below
- interaction: float32 [1536, 128, 128], P(('src', 'delay')), may hold values from -0.0546875 to 0.0546875
- pattern: int32 [3, 1536], P(None, ('src', 'delay')), may hold values from 0 to 15, as said below
- live: int32 [32], P(('src', 'delay')), may hold values from 12 to 48
- near_inverse: float32 [16, 128, 128], P('src'), may hold values from -0.5 to 0.5
- incident: float32 [4, 16, 16, 128], P(None, 'src'), may hold values from -6 to 6
Outputs:
- currents: float32 [4, 16, 16, 128], P(None, 'src')
Inputs may be any that keep to these rules, and one draw needn't show every extreme that they name: `slot_map`: each band's 4 entries are a cyclic rotation of 0 .. 3. `pattern`: row 0 lies in 0 .. 3, row 1 in 0 .. 15, row 2 in 0 .. 3.
All inputs are finite; a program needn't handle non-finite values.
Results may differ from a plain program's by a relative error of at most 0.0003.
Values sent between devices are 32-bit elements; how exact they have to be, the bound alone decides.
No kernel may reach another device: no remote copies, remote signals or barrier semaphores. Data moves between devices by JAX's collectives and lax.ppermute only.
A program may use at most 64 MiB of HBM per device.

v0:
```python
import jax
import jax.numpy as jnp
from jax import lax
from jax.sharding import PartitionSpec as P


def shifted(x, axis, by):
    devices = lax.axis_size(axis)
    pairs = [(i, i + by) for i in range(devices) if 0 <= i + by < devices]
    return lax.ppermute(x, axis, pairs)


def slot_holding(slot_map, wanted, moment):
    length = slot_map.shape[0]
    positions = jnp.arange(length, dtype=jnp.int32)
    return jnp.sum(jnp.where((slot_map + moment) % length == wanted, positions, 0))


def body(history, slot_map, interaction, pattern, live, near_inverse, incident):
    slot_count = history.shape[0]
    group_blocks = history.shape[1]
    columns = history.shape[2]
    block_width = history.shape[3]
    moments = incident.shape[0]
    pair_count = interaction.shape[0]
    positions = jnp.arange(slot_count, dtype=jnp.int32)
    at_front = lax.axis_index("delay") == 0
    in_use = (jnp.arange(pair_count, dtype=jnp.int32) < live[0]).astype(jnp.float32)
    row_match = pattern[0][None, :] == jnp.arange(group_blocks, dtype=jnp.int32)[:, None]
    selector = row_match.astype(jnp.float32) * in_use[None, :]
    band_state = lax.all_gather(history, "src", axis=1, tiled=True)
    results = []
    newest = None
    for moment in range(moments):
        if moment > 0:
            vacated = slot_holding(slot_map, slot_count - 1, moment - 1)
            outgoing_slot = lax.dynamic_index_in_dim(band_state, vacated, 0, keepdims=False)
            incoming = shifted(outgoing_slot, "delay", 1)
            entering = jnp.where(at_front, newest, incoming)
            band_state = lax.dynamic_update_index_in_dim(band_state, entering, vacated, 0)
        holder_match = (slot_map[None, :] + moment) % slot_count == pattern[2][:, None]
        holder = jnp.sum(jnp.where(holder_match, positions[None, :], 0), axis=1)
        picked = band_state[holder, pattern[1]]
        products = jnp.einsum("pab,prb->pra", interaction, picked, precision=lax.Precision.HIGHEST)
        partial_field = jnp.dot(
            selector,
            products.reshape(pair_count, columns * block_width),
            precision=lax.Precision.HIGHEST,
        )
        partial_field = partial_field.reshape(group_blocks, columns, block_width)
        field_sum = lax.psum(partial_field, "delay")
        current = jnp.einsum(
            "iab,irb->ira",
            near_inverse,
            incident[moment] - field_sum,
            precision=lax.Precision.HIGHEST,
        )
        results.append(current)
        if moment + 1 < moments:
            newest = lax.all_gather(current, "src", axis=0, tiled=True)
    return jnp.stack(results)


def solution(mesh):
    return jax.shard_map(
        body,
        mesh=mesh,
        in_specs=(
            P("delay", "src", None, None),
            P("delay"),
            P(("src", "delay"), None, None),
            P(None, ("src", "delay")),
            P(("src", "delay")),
            P("src", None, None),
            P(None, "src", None, None),
        ),
        out_specs=P(None, "src", None, None),
        check_vma=False,
    )
```

profile of v0, /device:TPU:4, one launch (start us, length us, event | category | flops | bytes accessed | tf_op | source)
XLA Modules:
  0.0 216.7 jit_solution(3523601571943106550)
XLA Ops:
  0.0 1.5 fusion.45
  1.5 18.1 %all_gather.12 = f32[4,16,16,128]{3,2,1,0:T(8,128)} all-gather(f32[4,4,16,128]{3,2,1,0:T(8,128)} %param.7), channel_id=1, replica_groups=mesh['src'=4,'delay'=8] {'src'}, dimensions={1}, use_global_device_ids=true | all-gather | bytes 655360 | tf_op jit(solution)/shard_map/all_gather | solution.py:31
  21.5 1.6 dynamic-slice_bitcast_fusion.2
  23.1 1.9 collective-permute-start
  25.0 0.8 slice_bitcast_fusion.1
  25.8 0.1 select_reduce_fusion
  25.9 0.7 fusion.64
  26.6 2.6 %gather_fusion = f32[48,16,128]{2,1,0:T(8,128)} fusion(f32[4,16,16,128]{3,2,1,0:T(8,128)} %all_gather.12, s32[48]{0:T(128)S(1)} %get-tuple-element.25), kind=kCustom, calls=%fused_computation | custom fusion | bytes 786816 | tf_op jit(solution)/shard_map/gather | solution.py:43
  29.9 0.0 copy-done
  29.9 0.0 copy-start.2
  29.9 6.0 %fusion.74 = f32[48,16,128]{2,1,0:T(8,128)S(1)} fusion(f32[48,16,128]{2,1,0:T(8,128)} %gather_fusion, f32[48,128,128]{2,1,0:T(8,128)S(1)} %copy-done), kind=kOutput, calls=%fused_computation.121 | convolution fusion | flops 150994944 | bytes 3932160 | tf_op jit(solution)/shard_map/pab,prb->pra/dot_general | solution.py:44
  35.8 0.0 copy-done.2
  35.8 0.4 fusion.9
  36.3 24.8 %psum.28 = f32[4,16,128]{2,0,1:T(4,128)S(1)} all-reduce(f32[4,16,128]{2,0,1:T(4,128)S(1)} %fusion.9), channel_id=1, replica_groups=mesh['src'=4,'delay'=8] {'delay'}, use_global_device_ids=true, to_apply=%region_1.2 | all-reduce | flops 8192 | bytes 65536 | tf_op jit(solution)/shard_map/psum | solution.py:51
  61.1 1.4 fusion.73
  62.5 0.0 copy-done.1
  62.5 0.0 copy-start.3
  62.5 0.5 fusion.21
  66.7 13.4 %all_gather.13 = f32[16,16,128]{2,1,0:T(8,128)S(1)} all-gather(f32[4,16,128]{2,1,0:T(8,128)S(1)} %fusion.21), channel_id=1, replica_groups=mesh['src'=4,'delay'=8] {'src'}, dimensions={0}, use_global_device_ids=true | all-gather | bytes 163840 | tf_op jit(solution)/shard_map/all_gather | solution.py:60
  80.0 0.0 collective-permute-done
  80.0 1.6 bitcast_dynamic-update-slice_fusion.2
  81.6 2.6 %gather_fusion.1 = f32[48,16,128]{2,1,0:T(8,128)} fusion(f32[4,16,16,128]{3,2,1,0:T(8,128)} %bitcast_dynamic-update-slice_fusion.2, s32[48]{0:T(128)S(1)} %get-tuple-element.24), kind=kCustom, calls=%fused_computation.1 | custom fusion | bytes 786816 | tf_op jit(solution)/shard_map/gather | solution.py:43
  84.3 6.0 %fusion.75 = f32[48,16,128]{2,1,0:T(8,128)S(1)} fusion(f32[48,16,128]{2,1,0:T(8,128)} %gather_fusion.1, f32[48,128,128]{2,1,0:T(8,128)S(1)} %copy-done), kind=kOutput, calls=%fused_computation.122 | convolution fusion | flops 150994944 | bytes 3932160 | tf_op jit(solution)/shard_map/pab,prb->pra/dot_general | solution.py:44
  90.2 1.0 fusion.6
  91.3 22.9 %psum.29 = f32[4,16,128]{2,0,1:T(4,128)S(1)} all-reduce(f32[4,16,128]{2,0,1:T(4,128)} %fusion.6), channel_id=1, replica_groups=mesh['src'=4,'delay'=8] {'delay'}, use_global_device_ids=true, to_apply=%region_4.5 | all-reduce | flops 8192 | bytes 65536 | tf_op jit(solution)/shard_map/psum | solution.py:51
  114.2 0.9 dynamic-slice_bitcast_fusion.1
  115.1 1.9 collective-permute-start.1
  117.0 0.5 fusion.19
  117.6 13.9 %all_gather.14 = f32[16,16,128]{2,1,0:T(8,128)S(1)} all-gather(f32[4,16,128]{2,1,0:T(8,128)S(1)} %fusion.19), channel_id=1, replica_groups=mesh['src'=4,'delay'=8] {'src'}, dimensions={0}, use_global_device_ids=true | all-gather | bytes 163840 | tf_op jit(solution)/shard_map/all_gather | solution.py:60
  131.4 0.0 collective-permute-done.1
  131.4 0.7 bitcast_dynamic-update-slice_fusion.1
  132.1 2.6 %gather_fusion.2 = f32[48,16,128]{2,1,0:T(8,128)} fusion(f32[4,16,16,128]{3,2,1,0:T(8,128)} %bitcast_dynamic-update-slice_fusion.1, s32[48]{0:T(128)S(1)} %get-tuple-element.23), kind=kCustom, calls=%fused_computation.2 | custom fusion | bytes 786816 | tf_op jit(solution)/shard_map/gather | solution.py:43
  134.7 6.0 %fusion.76 = f32[48,16,128]{2,1,0:T(8,128)S(1)} fusion(f32[48,16,128]{2,1,0:T(8,128)} %gather_fusion.2, f32[48,128,128]{2,1,0:T(8,128)S(1)} %copy-done), kind=kOutput, calls=%fused_computation.123 | convolution fusion | flops 150994944 | bytes 3932160 | tf_op jit(solution)/shard_map/pab,prb->pra/dot_general | solution.py:44
  140.7 1.0 fusion.3
  141.7 22.9 %psum.30 = f32[4,16,128]{2,0,1:T(4,128)S(1)} all-reduce(f32[4,16,128]{2,0,1:T(4,128)} %fusion.3), channel_id=1, replica_groups=mesh['src'=4,'delay'=8] {'delay'}, use_global_device_ids=true, to_apply=%region_7.8 | all-reduce | flops 8192 | bytes 65536 | tf_op jit(solution)/shard_map/psum | solution.py:51
  164.6 0.9 dynamic-slice_bitcast_fusion
  165.6 1.9 collective-permute-start.2
  167.5 0.5 fusion.17
  168.0 13.5 %all_gather.15 = f32[16,16,128]{2,1,0:T(8,128)S(1)} all-gather(f32[4,16,128]{2,1,0:T(8,128)S(1)} %fusion.17), channel_id=1, replica_groups=mesh['src'=4,'delay'=8] {'src'}, dimensions={0}, use_global_device_ids=true | all-gather | bytes 163840 | tf_op jit(solution)/shard_map/all_gather | solution.py:60
  181.6 0.0 collective-permute-done.2
  181.6 0.7 bitcast_dynamic-update-slice_fusion
  182.2 2.6 %gather_fusion.3 = f32[48,16,128]{2,1,0:T(8,128)} fusion(f32[4,16,16,128]{3,2,1,0:T(8,128)} %bitcast_dynamic-update-slice_fusion, s32[48]{0:T(128)S(1)} %get-tuple-element.9), kind=kCustom, calls=%fused_computation.3 | custom fusion | bytes 786816 | tf_op jit(solution)/shard_map/gather | solution.py:43
  184.9 6.0 %fusion.77 = f32[48,16,128]{2,1,0:T(8,128)S(1)} fusion(f32[48,16,128]{2,1,0:T(8,128)} %gather_fusion.3, f32[48,128,128]{2,1,0:T(8,128)S(1)} %copy-done), kind=kOutput, calls=%fused_computation.124 | convolution fusion | flops 150994944 | bytes 3932160 | tf_op jit(solution)/shard_map/pab,prb->pra/dot_general | solution.py:44
  190.8 1.0 fusion
  191.9 22.9 %psum.31 = f32[4,16,128]{2,0,1:T(4,128)S(1)} all-reduce(f32[4,16,128]{2,0,1:T(4,128)} %fusion), channel_id=1, replica_groups=mesh['src'=4,'delay'=8] {'delay'}, use_global_device_ids=true, to_apply=%region_10.11 | all-reduce | flops 8192 | bytes 65536 | tf_op jit(solution)/shard_map/psum | solution.py:51
  214.8 0.8 fusion.12
  215.5 0.5 convolution_bitcast_fusion
  216.0 0.7 pad_maximum_fusion
  (10 shorter events, 0.1 us)
Async XLA Ops:
  0.0 29.9 %copy-start = (f32[48,128,128]{2,1,0:T(8,128)S(1)}, f32[48,128,128]{2,1,0:T(8,128)}, u32[]{:S(2)}) copy-start(f32[48,128,128]{2,1,0:T(8,128)} %param.9) | copy-start | bytes 9437188
  1.5 61.0 %copy-start.1 = (f32[4,128,128]{2,1,0:T(8,128)S(1)}, f32[4,128,128]{2,1,0:T(8,128)}, u32[]{:S(2)}) copy-start(f32[4,128,128]{2,1,0:T(8,128)} %param.12) | copy-start | bytes 786436
  23.1 56.9 %collective-permute-start = (f32[16,16,128]{2,1,0:T(8,128)}, f32[16,16,128]{2,1,0:T(8,128)}, u32[]{:S(2)}, u32[]{:S(2)}) collective-permute-start(f32[16,16,128]{2,1,0:T(8,128)} %dynamic-slice_bitcast_fusion.2), channel_id=1, source_target_pairs={{0,1},{1,2},{2,3},{3,4},{4,5},{5,6},{6,7},{8,9},{9,10},{10,11},{11... | collective-permute-start | bytes 393224 | tf_op jit(solution)/shard_map/ppermute | solution.py:10
  29.9 6.0 %copy-start.2 = (f32[48]{0:T(128)}, f32[48]{0:T(128)S(1)}, u32[]{:S(2)}) copy-start(f32[48]{0:T(128)S(1)} %compare_convert_fusion) | copy-start | bytes 580
  62.5 27.7 %copy-start.3 = (f32[48]{0:T(128)S(1)}, f32[48]{0:T(128)}, u32[]{:S(2)}) copy-start(f32[48]{0:T(128)} %copy-done.2) | copy-start | bytes 580
  90.2 50.5 %copy-start.4 = (f32[48]{0:T(128)S(1)}, f32[48]{0:T(128)}, u32[]{:S(2)}) copy-start(f32[48]{0:T(128)} %copy-done.2) | copy-start | bytes 580
  115.1 16.3 %collective-permute-start.1 = (f32[16,16,128]{2,1,0:T(8,128)S(1)}, f32[16,16,128]{2,1,0:T(8,128)S(1)}, u32[]{:S(2)}, u32[]{:S(2)}) collective-permute-start(f32[16,16,128]{2,1,0:T(8,128)S(1)} %dynamic-slice_bitcast_fusion.1), channel_id=1, source_target_pairs={{0,1},{1,2},{2,3},{3,4},{4,5},{5,6},{6,7},{8,9},{9,10},{10,11},{11... | collective-permute-start | bytes 393224 | tf_op jit(solution)/shard_map/ppermute | solution.py:10
  165.6 16.0 %collective-permute-start.2 = (f32[16,16,128]{2,1,0:T(8,128)S(1)}, f32[16,16,128]{2,1,0:T(8,128)S(1)}, u32[]{:S(2)}, u32[]{:S(2)}) collective-permute-start(f32[16,16,128]{2,1,0:T(8,128)S(1)} %dynamic-slice_bitcast_fusion), channel_id=1, source_target_pairs={{0,1},{1,2},{2,3},{3,4},{4,5},{5,6},{6,7},{8,9},{9,10},{10,11},{11... | collective-permute-start | bytes 393224 | tf_op jit(solution)/shard_map/ppermute | solution.py:10
where the time goes:
time: 218 us; the launch traced here: 217 us
  blocking collectives  152 us (70%)
  matrix products  29.4 us (13%)
  local copies, waits for them, and re-layouts  16.2 us (7%)
  other arithmetic  6.73 us (3%)
  between operations  6.34 us (3%)
  starting transfers between devices  5.75 us (3%)
    psum x4, blocking collectives, body(): field_sum = lax.psum(partial_field, 'delay')  93.5 us
    all_gather x3, blocking collectives, body(): newest = lax.all_gather(current, 'src', axis=0, tiled=True)  40.7 us
    dot_general x4, matrix products, body(): jnp.einsum('pab,prb->pra', interaction, picked, precision=lax.Precision.H...  23.8 us
    all_gather x1, blocking collectives, body(): band_state = lax.all_gather(history, 'src', axis=1, tiled=True)  18.1 us
    gather x4, local copies, waits for them, and re-layouts, body(): picked = band_state[holder, pattern[1]]  10.6 us
    ppermute x3, starting transfers between devices, shifted(): return lax.ppermute(x, axis, pairs)  5.75 us
  transfers between devices with their start and end apart: 3, of which 0 were waited for; matrix products, arithmetic and copies ran while one was open for 6% of the time, Pallas kernels for 0%

commit v1 on v0

--- a/solution.py
+++ b/solution.py
@@ -28,7 +28,14 @@
     in_use = (jnp.arange(pair_count, dtype=jnp.int32) < live[0]).astype(jnp.float32)
     row_match = pattern[0][None, :] == jnp.arange(group_blocks, dtype=jnp.int32)[:, None]
     selector = row_match.astype(jnp.float32) * in_use[None, :]
-    band_state = lax.all_gather(history, "src", axis=1, tiled=True)
+    n_dev = lax.axis_size("src")
+    hops = [(i_2, (i_2 + 1) % n_dev) for i_2 in range(n_dev)]
+    parts = [history]
+    for far in range(1, n_dev):
+        parts = [lax.ppermute(parts[0], "src", hops), *parts]
+    result = jnp.concatenate(parts, axis=1)
+    offset = (lax.axis_index("src") + 1) * parts[-1].shape[1]
+    band_state = jnp.roll(result, offset, axis=1)
     results = []
     newest = None
     for moment in range(moments):

time: 218 us -> 209 us (0.959)
  blocking collectives: 152 us -> 131 us
  waiting for transfers between devices: 0.01 us -> 7.56 us
  local copies, waits for them, and re-layouts: 16.2 us -> 19.7 us
    all_gather x1 -> x0, blocking collectives: 18.1 us -> none  [body(): band_state = lax.all_gather(history, 'src', axis=1, tiled=True)]
    ppermute x0 -> x3, waiting for transfers between devices: none -> 7.55 us  [body(): parts = [lax.ppermute(parts[0], 'src', hops), *parts]]
    psum x4, blocking collectives: 93.5 us -> 90.7 us  [body(): field_sum = lax.psum(partial_field, 'delay')]
  transfers between devices with their start and end apart: 3 -> 6, of which waited for: 0 -> 2; matrix products, arithmetic and copies ran while one was open for 6% -> 3% of each run, Pallas kernels for 0% -> 0%
where the time goes in v1:
time: 209 us; the launch traced here: 208 us
  blocking collectives  131 us (63%)
  matrix products  29.5 us (14%)
  local copies, waits for them, and re-layouts  19.7 us (9%)
  waiting for transfers between devices  7.56 us (4%)
  starting transfers between devices  7.42 us (4%)
  between operations  6.53 us (3%)
  other arithmetic  6.27 us (3%)
    psum x4, blocking collectives, body(): field_sum = lax.psum(partial_field, 'delay')  90.7 us
    all_gather x3, blocking collectives, body(): newest = lax.all_gather(current, 'src', axis=0, tiled=True)  40.4 us
    dot_general x4, matrix products, body(): jnp.einsum('pab,prb->pra', interaction, picked, precision=lax.Precision.H...  23.8 us
    gather x4, local copies, waits for them, and re-layouts, body(): picked = band_state[holder, pattern[1]]  10.5 us
    ppermute x3, waiting for transfers between devices, body(): parts = [lax.ppermute(parts[0], 'src', hops), *parts]  7.55 us
    ppermute x3, starting transfers between devices, shifted(): return lax.ppermute(x, axis, pairs)  5.76 us
  transfers between devices with their start and end apart: 6, of which 2 were waited for; matrix products, arithmetic and copies ran while one was open for 3% of the time, Pallas kernels for 0%

profile of v1, /device:TPU:4, one launch (start us, length us, event | category | flops | bytes accessed | tf_op | source)
XLA Modules:
  0.0 208.0 jit_solution(6803474781616929520)
XLA Ops:
  0.0 1.6 collective-permute-start
  1.6 1.3 slice_bitcast_fusion.1
  2.8 1.4 fusion.73
  4.3 1.4 fusion.45
  5.7 0.1 select_reduce_fusion
  5.8 1.6 collective-permute-done
  7.3 0.1 collective-permute-start.1
  7.4 0.7 fusion.64
  8.1 6.0 %collective-permute-done.1 = f32[4,4,16,128]{3,2,1,0:T(8,128)S(1)} collective-permute-done((f32[4,4,16,128]{3,2,1,0:T(8,128)S(1)}, f32[4,4,16,128]{3,2,1,0:T(8,128)S(1)}, u32[]{:S(2)}, u32[]{:S(2)}) %collective-permute-start.1) | collective-permute-done | bytes 131104 | tf_op jit(solution)/shard_map/ppermute | solution.py:35
  20.4 0.6 compare_convert_fusion
  21.1 0.9 constant_dynamic-update-slice_fusion.4
  22.1 0.9 constant_dynamic-update-slice_fusion
  23.0 1.0 copy-done.2
  24.0 0.9 constant_dynamic-slice_fusion
  24.8 2.6 %gather_fusion = f32[48,16,128]{2,1,0:T(8,128)} fusion(f32[4,16,16,128]{3,2,1,0:T(8,128)} %constant_dynamic-slice_fusion, s32[48]{0:T(128)S(1)} %get-tuple-element.25), kind=kCustom, calls=%fused_computation | custom fusion | bytes 786816 | tf_op jit(solution)/shard_map/gather | solution.py:50
  27.4 6.0 %fusion.74 = f32[48,16,128]{2,1,0:T(8,128)S(1)} fusion(f32[48,16,128]{2,1,0:T(8,128)} %gather_fusion, f32[48,128,128]{2,1,0:T(8,128)S(1)} %copy-done), kind=kOutput, calls=%fused_computation.130 | convolution fusion | flops 150994944 | bytes 3932160 | tf_op jit(solution)/shard_map/pab,prb->pra/dot_general | solution.py:51
  33.4 0.4 fusion.9
  33.8 22.4 %psum.28 = f32[4,16,128]{2,0,1:T(4,128)S(1)} all-reduce(f32[4,16,128]{2,0,1:T(4,128)S(1)} %fusion.9), channel_id=1, replica_groups=mesh['src'=4,'delay'=8] {'delay'}, use_global_device_ids=true, to_apply=%region_1.2 | all-reduce | flops 8192 | bytes 65536 | tf_op jit(solution)/shard_map/psum | solution.py:58
  56.2 0.9 dynamic-slice_bitcast_fusion.2
  57.1 1.9 collective-permute-start.3
  59.1 0.5 fusion.21
  59.6 13.4 %all_gather.9 = f32[16,16,128]{2,1,0:T(8,128)S(1)} all-gather(f32[4,16,128]{2,1,0:T(8,128)S(1)} %fusion.21), channel_id=1, replica_groups=mesh['src'=4,'delay'=8] {'src'}, dimensions={0}, use_global_device_ids=true | all-gather | bytes 163840 | tf_op jit(solution)/shard_map/all_gather | solution.py:67
  73.0 0.7 bitcast_dynamic-update-slice_fusion.2
  73.7 2.6 %gather_fusion.1 = f32[48,16,128]{2,1,0:T(8,128)} fusion(f32[4,16,16,128]{3,2,1,0:T(8,128)} %bitcast_dynamic-update-slice_fusion.2, s32[48]{0:T(128)S(1)} %get-tuple-element.24), kind=kCustom, calls=%fused_computation.1 | custom fusion | bytes 786816 | tf_op jit(solution)/shard_map/gather | solution.py:50
  76.3 6.0 %fusion.75 = f32[48,16,128]{2,1,0:T(8,128)S(1)} fusion(f32[48,16,128]{2,1,0:T(8,128)} %gather_fusion.1, f32[48,128,128]{2,1,0:T(8,128)S(1)} %copy-done), kind=kOutput, calls=%fused_computation.131 | convolution fusion | flops 150994944 | bytes 3932160 | tf_op jit(solution)/shard_map/pab,prb->pra/dot_general | solution.py:51
  82.2 1.2 fusion.6
  83.4 22.4 %psum.29 = f32[4,16,128]{2,0,1:T(4,128)S(1)} all-reduce(f32[4,16,128]{2,0,1:T(4,128)S(1)} %fusion.6), channel_id=1, replica_groups=mesh['src'=4,'delay'=8] {'delay'}, use_global_device_ids=true, to_apply=%region_4.5 | all-reduce | flops 8192 | bytes 65536 | tf_op jit(solution)/shard_map/psum | solution.py:58
  105.8 0.9 dynamic-slice_bitcast_fusion.1
  106.7 1.9 collective-permute-start.4
  108.7 0.5 fusion.19
  109.2 13.6 %all_gather.10 = f32[16,16,128]{2,1,0:T(8,128)S(1)} all-gather(f32[4,16,128]{2,1,0:T(8,128)S(1)} %fusion.19), channel_id=1, replica_groups=mesh['src'=4,'delay'=8] {'src'}, dimensions={0}, use_global_device_ids=true | all-gather | bytes 163840 | tf_op jit(solution)/shard_map/all_gather | solution.py:67
  122.8 0.7 bitcast_dynamic-update-slice_fusion.1
  123.4 2.6 %gather_fusion.2 = f32[48,16,128]{2,1,0:T(8,128)} fusion(f32[4,16,16,128]{3,2,1,0:T(8,128)} %bitcast_dynamic-update-slice_fusion.1, s32[48]{0:T(128)S(1)} %get-tuple-element.23), kind=kCustom, calls=%fused_computation.2 | custom fusion | bytes 786816 | tf_op jit(solution)/shard_map/gather | solution.py:50
  126.0 6.0 %fusion.76 = f32[48,16,128]{2,1,0:T(8,128)S(1)} fusion(f32[48,16,128]{2,1,0:T(8,128)} %gather_fusion.2, f32[48,128,128]{2,1,0:T(8,128)S(1)} %copy-done), kind=kOutput, calls=%fused_computation.132 | convolution fusion | flops 150994944 | bytes 3932160 | tf_op jit(solution)/shard_map/pab,prb->pra/dot_general | solution.py:51
  132.0 1.0 fusion.3
  133.0 23.0 %psum.30 = f32[4,16,128]{2,0,1:T(4,128)S(1)} all-reduce(f32[4,16,128]{2,0,1:T(4,128)} %fusion.3), channel_id=1, replica_groups=mesh['src'=4,'delay'=8] {'delay'}, use_global_device_ids=true, to_apply=%region_7.8 | all-reduce | flops 8192 | bytes 65536 | tf_op jit(solution)/shard_map/psum | solution.py:58
  156.0 0.9 dynamic-slice_bitcast_fusion
  156.9 1.9 collective-permute-start.5
  158.9 0.5 fusion.17
  159.4 13.4 %all_gather.11 = f32[16,16,128]{2,1,0:T(8,128)S(1)} all-gather(f32[4,16,128]{2,1,0:T(8,128)S(1)} %fusion.17), channel_id=1, replica_groups=mesh['src'=4,'delay'=8] {'src'}, dimensions={0}, use_global_device_ids=true | all-gather | bytes 163840 | tf_op jit(solution)/shard_map/all_gather | solution.py:67
  172.8 0.7 bitcast_dynamic-update-slice_fusion
  173.4 2.6 %gather_fusion.3 = f32[48,16,128]{2,1,0:T(8,128)} fusion(f32[4,16,16,128]{3,2,1,0:T(8,128)} %bitcast_dynamic-update-slice_fusion, s32[48]{0:T(128)S(1)} %get-tuple-element.9), kind=kCustom, calls=%fused_computation.3 | custom fusion | bytes 786816 | tf_op jit(solution)/shard_map/gather | solution.py:50
  176.1 6.0 %fusion.77 = f32[48,16,128]{2,1,0:T(8,128)S(1)} fusion(f32[48,16,128]{2,1,0:T(8,128)} %gather_fusion.3, f32[48,128,128]{2,1,0:T(8,128)S(1)} %copy-done), kind=kOutput, calls=%fused_computation.133 | convolution fusion | flops 150994944 | bytes 3932160 | tf_op jit(solution)/shard_map/pab,prb->pra/dot_general | solution.py:51
  182.0 1.0 fusion
  183.0 23.0 %psum.31 = f32[4,16,128]{2,0,1:T(4,128)S(1)} all-reduce(f32[4,16,128]{2,0,1:T(4,128)} %fusion), channel_id=1, replica_groups=mesh['src'=4,'delay'=8] {'delay'}, use_global_device_ids=true, to_apply=%region_10.11 | all-reduce | flops 8192 | bytes 65536 | tf_op jit(solution)/shard_map/psum | solution.py:58
  206.0 0.8 fusion.12
  206.8 0.5 convolution_bitcast_fusion
  207.3 0.7 pad_maximum_fusion
  (32 shorter events, 0.2 us)
Async XLA Ops:
  0.0 27.4 %copy-start = (f32[48,128,128]{2,1,0:T(8,128)S(1)}, f32[48,128,128]{2,1,0:T(8,128)}, u32[]{:S(2)}) copy-start(f32[48,128,128]{2,1,0:T(8,128)} %param.9) | copy-start | bytes 9437188
  0.0 7.3 %collective-permute-start = (f32[4,4,16,128]{3,2,1,0:T(8,128)}, f32[4,4,16,128]{3,2,1,0:T(8,128)S(1)}, u32[]{:S(2)}, u32[]{:S(2)}) collective-permute-start(f32[4,4,16,128]{3,2,1,0:T(8,128)} %param.7), channel_id=1, source_target_pairs={{0,8},{8,16},{16,24},{24,0},{1,9},{9,17},{17,25},{25,1},{2,10},{10... | collective-permute-start | bytes 393224 | tf_op jit(solution)/shard_map/ppermute | solution.py:35
  7.3 6.8 %collective-permute-start.1 = (f32[4,4,16,128]{3,2,1,0:T(8,128)S(1)}, f32[4,4,16,128]{3,2,1,0:T(8,128)S(1)}, u32[]{:S(2)}, u32[]{:S(2)}) collective-permute-start(f32[4,4,16,128]{3,2,1,0:T(8,128)S(1)} %collective-permute-done), channel_id=1, source_target_pairs={{0,8},{8,16},{16,24},{24,0},{1,9},{9,17},{17,25},{25,1},{2,10},{10... | collective-permute-start | bytes 393224 | tf_op jit(solution)/shard_map/ppermute | solution.py:35
  14.1 6.9 %collective-permute-start.2 = (f32[4,4,16,128]{3,2,1,0:T(8,128)S(1)}, f32[4,4,16,128]{3,2,1,0:T(8,128)S(1)}, u32[]{:S(2)}, u32[]{:S(2)}) collective-permute-start(f32[4,4,16,128]{3,2,1,0:T(8,128)S(1)} %collective-permute-done.1), channel_id=1, source_target_pairs={{0,8},{8,16},{16,24},{24,0},{1,9},{9,17},{17,25},{25,1},{2,10},{10... | collective-permute-start | bytes 393224 | tf_op jit(solution)/shard_map/ppermute | solution.py:35
  22.0 11.4 %copy-start.6 = (s32[48]{0:T(128)S(1)}, s32[48]{0:T(128)}, u32[]{:S(2)}) copy-start(s32[48]{0:T(128)} %get-tuple-element.21) | copy-start | bytes 580
  22.0 11.4 %copy-start.7 = (f32[48]{0:T(128)S(1)}, f32[48]{0:T(128)}, u32[]{:S(2)}) copy-start(f32[48]{0:T(128)} %compare_convert_fusion) | copy-start | bytes 580
  23.0 1.0 copy-start.2
  24.0 35.1 %copy-start.5 = (f32[1,4,16,128]{3,2,1,0:T(8,128)S(1)}, f32[1,4,16,128]{3,2,1,0:T(8,128)}, u32[]{:S(2)}) copy-start(f32[1,4,16,128]{3,2,1,0:T(8,128)} %get-tuple-element.20) | copy-start | bytes 98308
  24.0 35.1 %copy-start.1 = (f32[4,128,128]{2,1,0:T(8,128)S(1)}, f32[4,128,128]{2,1,0:T(8,128)}, u32[]{:S(2)}) copy-start(f32[4,128,128]{2,1,0:T(8,128)} %param.12) | copy-start | bytes 786436
  57.1 15.9 %collective-permute-start.3 = (f32[16,16,128]{2,1,0:T(8,128)S(1)}, f32[16,16,128]{2,1,0:T(8,128)S(1)}, u32[]{:S(2)}, u32[]{:S(2)}) collective-permute-start(f32[16,16,128]{2,1,0:T(8,128)S(1)} %dynamic-slice_bitcast_fusion.2), channel_id=1, source_target_pairs={{0,1},{1,2},{2,3},{3,4},{4,5},{5,6},{6,7},{8,9},{9,10},{10,11},{11... | collective-permute-start | bytes 393224 | tf_op jit(solution)/shard_map/ppermute | solution.py:10
  59.1 49.5 %copy-start.4 = (f32[1,4,16,128]{3,2,1,0:T(8,128)S(1)}, f32[1,4,16,128]{3,2,1,0:T(8,128)}, u32[]{:S(2)}) copy-start(f32[1,4,16,128]{3,2,1,0:T(8,128)} %get-tuple-element.19) | copy-start | bytes 98308
  82.2 49.8 %copy-start.8 = (f32[48]{0:T(128)S(1)}, f32[48]{0:T(128)}, u32[]{:S(2)}) copy-start(f32[48]{0:T(128)} %compare_convert_fusion) | copy-start | bytes 580
  106.7 16.1 %collective-permute-start.4 = (f32[16,16,128]{2,1,0:T(8,128)S(1)}, f32[16,16,128]{2,1,0:T(8,128)S(1)}, u32[]{:S(2)}, u32[]{:S(2)}) collective-permute-start(f32[16,16,128]{2,1,0:T(8,128)S(1)} %dynamic-slice_bitcast_fusion.1), channel_id=1, source_target_pairs={{0,1},{1,2},{2,3},{3,4},{4,5},{5,6},{6,7},{8,9},{9,10},{10,11},{11... | collective-permute-start | bytes 393224 | tf_op jit(solution)/shard_map/ppermute | solution.py:10
  108.7 50.2 %copy-start.3 = (f32[1,4,16,128]{3,2,1,0:T(8,128)S(1)}, f32[1,4,16,128]{3,2,1,0:T(8,128)}, u32[]{:S(2)}) copy-start(f32[1,4,16,128]{3,2,1,0:T(8,128)} %get-tuple-element.18) | copy-start | bytes 98308
  156.9 15.9 %collective-permute-start.5 = (f32[16,16,128]{2,1,0:T(8,128)S(1)}, f32[16,16,128]{2,1,0:T(8,128)S(1)}, u32[]{:S(2)}, u32[]{:S(2)}) collective-permute-start(f32[16,16,128]{2,1,0:T(8,128)S(1)} %dynamic-slice_bitcast_fusion), channel_id=1, source_target_pairs={{0,1},{1,2},{2,3},{3,4},{4,5},{5,6},{6,7},{8,9},{9,10},{10,11},{11... | collective-permute-start | bytes 393224 | tf_op jit(solution)/shard_map/ppermute | solution.py:10
